TPU v7x, 32 devices: a whole 2x2x4 slice. The times are simulated.
32 devices in a mesh: parts: 2 (over y), mp: 4 (over z), dp: 4 (over x, core).
Axes of the slice: x: 2, y: 2, z: 4, core: 2. Of those that a mesh axis runs over, the one named last changes fastest.
Arguments:
- embeddings: bfloat16 [2048, 1024], P(('parts', 'dp')), parts along dimension 0, may hold values from -16 to 16
- w_in: bfloat16 [1024, 8192], P(None, 'mp'), may hold values from -0.1875 to 0.1875
- w_out: bfloat16 [8192, 1024], P('mp'), may hold values from -0.0625 to 0.0625
- means: bfloat16 [8192, 1024], P('mp'), may hold values from -2.09375 to 2.09375
- precisions: bfloat16 [8192, 1024], P('mp'), may hold values from 0.04 to 0.16
- log_weight: float32 [8192], P('mp'), may hold values from -4 to 0
Outputs:
- counts: float32 [16384], P(('parts', 'mp')), parts along dimension 0
- first_moment: float32 [2048, 8192], P(('parts', 'dp'), 'mp'), parts along dimension 0
- second_moment: float32 [2048, 8192], P(('parts', 'dp'), 'mp'), parts along dimension 0
- grad_w_in: bfloat16 [2048, 8192], P(('parts', 'dp'), 'mp'), parts along dimension 0
- grad_w_out_t: bfloat16 [2048, 8192], P(('parts', 'dp'), 'mp'), parts along dimension 0
- grad_embed: bfloat16 [2048, 1024], P(('parts', 'dp')), parts along dimension 0
There are 2 independent parts, one for each index of `parts`. A program takes and returns all parts, laid end to end along the dimension named above; an argument that names none is the same for every part. Nothing has to cross between parts.
All inputs are finite; a program needn't handle non-finite values.
Results may differ from a plain program's by a relative error of at most 0.028.
Values may be sent and summed in bfloat16 or wider, within the bound.
A program may use at most 128 MiB of HBM per device.

v0:
```python
import jax
import jax.numpy as jnp
from jax import lax
from jax.sharding import PartitionSpec as P


def my_columns(rows, axis):
    gathered = lax.all_gather(rows, axis, axis=0, tiled=True)
    width = rows.shape[1] // lax.axis_size(axis)
    return lax.dynamic_slice_in_dim(gathered, lax.axis_index(axis) * width, width, 1)


def body(embeddings, w_in, w_out, means, precisions, log_weight):
    contract_rows = (((0,), (0,)), ((), ()))
    contract_cols = (((1,), (1,)), ((), ()))
    pre = jnp.dot(embeddings, w_in, preferred_element_type=jnp.float32)
    hidden = jax.nn.silu(pre).astype(jnp.bfloat16)
    hidden_all = lax.all_gather(hidden, "dp", axis=0, tiled=True)
    emb_cols = my_columns(embeddings, "dp")
    partial_value = jnp.dot(hidden, w_out, preferred_element_type=jnp.float32)
    head = lax.psum(partial_value, "mp").astype(jnp.bfloat16)
    head_f = head.astype(jnp.float32)
    squares = (head_f * head_f).astype(jnp.bfloat16)
    means_f = means.astype(jnp.float32)
    prec_f = precisions.astype(jnp.float32)
    weighted = (means_f * prec_f).astype(jnp.bfloat16)
    offset = (
        log_weight
        + 0.5 * jnp.sum(jnp.log(prec_f), axis=1)
        - 0.5 * jnp.sum(means_f * means_f * prec_f, axis=1)
    )
    scores = offset[None, :] + lax.dot_general(
        head, weighted, contract_cols, preferred_element_type=jnp.float32
    )
    scores = scores - 0.5 * lax.dot_general(
        squares, precisions, contract_cols, preferred_element_type=jnp.float32
    )
    local_top = jnp.max(scores, axis=1)
    local_total = jnp.sum(jnp.exp(scores - local_top[:, None]), axis=1)
    stats = lax.all_gather(jnp.stack([local_top, local_total]), "mp")
    top = jnp.max(stats[:, 0], axis=0)
    total = jnp.sum(stats[:, 1] * jnp.exp(stats[:, 0] - top), axis=0)
    lse = top + jnp.log(total)
    resp = jnp.exp(scores - lse[:, None])
    resp_b = resp.astype(jnp.bfloat16)
    counts = lax.psum(jnp.sum(resp, axis=0), "dp")
    resp_all = lax.all_gather(resp_b, "dp", axis=0, tiled=True)
    head_cols = my_columns(head, "dp")
    head_cols_f = head_cols.astype(jnp.float32)
    squares_cols = (head_cols_f * head_cols_f).astype(jnp.bfloat16)
    first_moment = lax.dot_general(
        head_cols, resp_all, contract_rows, preferred_element_type=jnp.float32
    )
    second_moment = lax.dot_general(
        squares_cols, resp_all, contract_rows, preferred_element_type=jnp.float32
    )
    along = jnp.dot(resp_b, precisions, preferred_element_type=jnp.float32)
    shifted = jnp.dot(resp_b, weighted, preferred_element_type=jnp.float32)
    grad_term = head_f * along - shifted
    grad_head = lax.psum(grad_term.astype(jnp.bfloat16), "mp")
    back = lax.dot_general(grad_head, w_out, contract_cols, preferred_element_type=jnp.float32)
    sigma = jax.nn.sigmoid(pre)
    grad_pre = (back * sigma * (1.0 + pre * (1.0 - sigma))).astype(jnp.bfloat16)
    embed_term = lax.dot_general(grad_pre, w_in, contract_cols, preferred_element_type=jnp.float32)
    grad_embed = lax.psum(embed_term.astype(jnp.bfloat16), "mp")
    pre_all = lax.all_gather(grad_pre, "dp", axis=0, tiled=True)
    grad_cols = my_columns(grad_head, "dp")
    grad_w_in = lax.dot_general(
        emb_cols, pre_all, contract_rows, preferred_element_type=jnp.float32
    ).astype(jnp.bfloat16)
    grad_w_out_t = lax.dot_general(
        grad_cols, hidden_all, contract_rows, preferred_element_type=jnp.float32
    ).astype(jnp.bfloat16)
    return (counts, first_moment, second_moment, grad_w_in, grad_w_out_t, grad_embed)


def solution(mesh):
    return jax.shard_map(
        body,
        mesh=mesh,
        in_specs=(
            P(("parts", "dp"), None),
            P(None, "mp"),
            P("mp", None),
            P("mp", None),
            P("mp", None),
            P("mp"),
        ),
        out_specs=(
            P(("parts", "mp")),
            P(("parts", "dp"), "mp"),
            P(("parts", "dp"), "mp"),
            P(("parts", "dp"), "mp"),
            P(("parts", "dp"), "mp"),
            P(("parts", "dp"), None),
        ),
        check_vma=False,
    )
```

profile of v0, /device:TPU:0, one launch (start us, length us, event | category | flops | bytes accessed | tf_op | source)
XLA Modules:
  0.0 288.4 jit_solution(5527400726379757286)
XLA Ops:
  8.0 5.0 %multiply_convert_fusion = (bf16[256,2048]{1,0:T(8,128)(2,1)S(1)}, f32[256,2048]{1,0:T(8,128)}) fusion(bf16[256,1024]{1,0:T(8,128)(2,1)} %param.6, bf16[1024,2048]{1,0:T(8,128)(2,1)} %param.7), kind=kOutput, calls=%fused_computation.17 | convolution fusion | flops 1076363264 | bytes 7864320 | tf_op jit(solution)/shard_map/dot_general | solution.py:16
  13.0 3.8 %fusion.34 = f32[256,1024]{1,0:T(8,128)S(1)} fusion(bf16[256,2048]{1,0:T(8,128)(2,1)S(1)} %get-tuple-element.13, bf16[2048,1024]{1,0:T(8,128)(2,1)} %param.8), kind=kOutput, calls=%fused_computation.50 | convolution fusion | flops 1073741824 | bytes 6291456 | tf_op jit(solution)/shard_map/dot_general | solution.py:20
  16.9 45.0 %all-reduce.7 = bf16[256,1024]{1,0:T(8,128)(2,1)S(1)} all-reduce(f32[256,1024]{1,0:T(8,128)S(1)} %fusion.34), channel_id=1, replica_groups=mesh['parts'=2,'mp'=4,'dp'=4] {'mp'}, use_global_device_ids=true, to_apply=%region_2.3 | all-reduce | flops 262144 | bytes 1572864 | tf_op jit(solution)/shard_map/psum | solution.py:21
  61.9 3.7 %convolution_multiply_fusion.1 = f32[256,2048]{1,0:T(8,128)S(1)} fusion(bf16[2048,1024]{1,0:T(8,128)(2,1)} %param.10, bf16[256,1024]{1,0:T(8,128)(2,1)S(1)} %all-reduce.7), kind=kOutput, calls=%fused_computation.8 | convolution fusion | flops 1075052544 | bytes 6815744 | tf_op jit(solution)/shard_map/dot_general | solution.py:35
  65.6 4.7 %fusion = (f32[2048]{0:T(1024)S(1)}, f32[2048]{0:T(1024)S(1)}) fusion(bf16[2048,1024]{1,0:T(8,128)(2,1)S(1)} %copy-done, bf16[2048,1024]{1,0:T(8,128)(2,1)} %param.9), kind=kLoop, calls=%fused_computation.4 | loop fusion | flops 12578816 | bytes 8404992 | tf_op jit(solution)/shard_map/reduce_sum | solution.py:29
  70.3 1.9 fusion.33
  72.7 11.9 %all-gather.1 = f32[4,2,256]{2,1,0:T(2,128)S(1)} all-gather(f32[1,2,256]{2,1,0:T(2,128)S(1)} %maximum_bitcast_fusion), channel_id=2, replica_groups=mesh['parts'=2,'mp'=4,'dp'=4] {'mp'}, dimensions={0}, use_global_device_ids=true | all-gather | bytes 10240 | tf_op jit(solution)/shard_map/all_gather | solution.py:40
  85.1 3.9 %convolution_multiply_fusion.2 = f32[256,1024]{1,0:T(8,128)S(1)} fusion(bf16[256,2048]{1,0:T(8,128)(2,1)S(1)} %get-tuple-element.8, bf16[2048,1024]{1,0:T(8,128)(2,1)} %param.10, bf16[256,1024]{1,0:T(8,128)(2,1)S(1)} %all-reduce.7), kind=kOutput, calls=%fused_computation.22 | convolution fusion | flops 1074266112 | bytes 6815744 | tf_op jit(solution)/shard_map/dot_general | solution.py:57
  89.0 4.6 %fusion.14 = bf16[256,1024]{1,0:T(8,128)(2,1)} fusion(f32[256,1024]{1,0:T(8,128)S(1)} %convolution_multiply_fusion.2, bf16[256,2048]{1,0:T(8,128)(2,1)S(1)} %get-tuple-element.8, bf16[2048,1024]{1,0:T(8,128)(2,1)S(1)} %copy-done.1, bf16[2048,1024]{1,0:T(8,128)(2,1)} %param.9), kind=kOutput, calls=%fused_computation.25 | convolution fusion | flops 1082654720 | bytes 11010048 | tf_op jit(solution)/shard_map/dot_general | solution.py:58
  94.9 36.3 %all-reduce.4.cloned.1.call-done = bf16[256,1024]{1,0:T(8,128)(2,1)} async-done(((bf16[256,1024]{1,0:T(8,128)(2,1)}), bf16[256,1024]{1,0:T(8,128)(2,1)}) %all-reduce.4.cloned.1.call-update) | async-done | bytes 524304 | tf_op jit(solution)/shard_map/psum | solution.py:60
  132.0 0.7 all-gather.13.cloned.1.call-update
  132.8 5.0 %fusion.5 = bf16[256,2048]{1,0:T(8,128)(2,1)} fusion(bf16[256,1024]{1,0:T(8,128)(2,1)} %all-reduce.4.cloned.1.call-done, bf16[2048,1024]{1,0:T(8,128)(2,1)} %param.8, f32[256,2048]{1,0:T(8,128)S(1)} %copy-done.8), kind=kOutput, calls=%fused_computation.12 | convolution fusion | flops 1078460416 | bytes 7864320 | tf_op jit(solution)/shard_map/dot_general | solution.py:61
  137.8 7.5 %psum.29 = f32[2048]{0:T(1024)} all-reduce(f32[2048]{0:T(1024)S(1)} %get-tuple-element.9), channel_id=1, replica_groups=mesh['parts'=2,'mp'=4,'dp'=4] {'dp'}, use_global_device_ids=true, to_apply=%region_8.9 | all-reduce | flops 2048 | bytes 16384 | tf_op jit(solution)/shard_map/psum | solution.py:46
  145.3 4.6 %convolution_convert_fusion.2 = bf16[256,1024]{1,0:T(8,128)(2,1)} fusion(bf16[256,2048]{1,0:T(8,128)(2,1)} %fusion.5, bf16[1024,2048]{1,0:T(8,128)(2,1)} %param.7), kind=kOutput, calls=%fused_computation.26 | convolution fusion | flops 1074003968 | bytes 5767168 | tf_op jit(solution)/shard_map/dot_general | solution.py:64
  150.0 4.2 %all-gather.11.cloned.1.call-done = bf16[1024,2048]{1,0:T(8,128)(2,1)} async-done(((bf16[256,2048]{1,0:T(8,128)(2,1)}), bf16[1024,2048]{1,0:T(8,128)(2,1)}) %all-gather.11.cloned.1.call-update) | async-done | bytes 4194320 | tf_op jit(solution)/shard_map/all_gather | solution.py:47
  154.2 5.2 %fusion.18 = f32[256,2048]{1,0:T(8,128)} fusion(bf16[1024,2048]{1,0:T(8,128)(2,1)} %all-gather.11.cloned.1.call-done, bf16[1024,1024]{1,0:T(8,128)(2,1)} %all-gather.9.cloned.1.call-done, s32[]{:T(128)S(6)} %select_n.2), kind=kOutput, calls=%fused_computation.29 | convolution fusion | flops 1074528256 | bytes 6815748 | tf_op jit(solution)/shard_map/dot_general | solution.py:54
  159.4 3.6 %fusion.23 = f32[256,2048]{1,0:T(8,128)} fusion(bf16[1024,2048]{1,0:T(8,128)(2,1)S(1)} %copy-done.7, bf16[1024,1024]{1,0:T(8,128)(2,1)} %all-gather.9.cloned.1.call-done, s32[]{:T(128)S(6)} %select_n.2), kind=kOutput, calls=%fused_computation.33 | convolution fusion | flops 1073741824 | bytes 6815748 | tf_op jit(solution)/shard_map/dot_general | solution.py:51
  163.0 15.1 %all-gather.17.cloned.1.call-done = bf16[1024,1024]{1,0:T(8,128)(2,1)} async-done(((bf16[256,1024]{1,0:T(8,128)(2,1)}), bf16[1024,1024]{1,0:T(8,128)(2,1)}) %all-gather.17.cloned.1.call-update) | async-done | bytes 2097168 | tf_op jit(solution)/shard_map/all_gather | solution.py:8
  178.0 35.9 %all-gather.19.cloned.1.call-done = bf16[1024,2048]{1,0:T(8,128)(2,1)} async-done(((bf16[256,2048]{1,0:T(8,128)(2,1)}), bf16[1024,2048]{1,0:T(8,128)(2,1)}) %all-gather.19.cloned.1.call-update) | async-done | bytes 4194320 | tf_op jit(solution)/shard_map/all_gather | solution.py:18
  214.0 4.6 %convolution_convert_fusion = bf16[256,2048]{1,0:T(8,128)(2,1)} fusion(bf16[1024,2048]{1,0:T(8,128)(2,1)} %all-gather.19.cloned.1.call-done, bf16[1024,1024]{1,0:T(8,128)(2,1)} %all-gather.17.cloned.1.call-done, s32[]{:T(128)S(6)} %select_n.2), kind=kOutput, calls=%fused_computation.13 | convolution fusion | flops 1074266112 | bytes 5767172 | tf_op jit(solution)/shard_map/dot_general | solution.py:71
  218.6 19.4 %all-gather.13.cloned.1.call-done = bf16[1024,1024]{1,0:T(8,128)(2,1)} async-done(((bf16[256,1024]{1,0:T(8,128)(2,1)}), bf16[1024,1024]{1,0:T(8,128)(2,1)}) %all-gather.13.cloned.1.call-update) | async-done | bytes 2097168 | tf_op jit(solution)/shard_map/all_gather | solution.py:8
  238.0 36.5 %all-gather.15.cloned.1.call-done = bf16[1024,2048]{1,0:T(8,128)(2,1)} async-done(((bf16[256,2048]{1,0:T(8,128)(2,1)}), bf16[1024,2048]{1,0:T(8,128)(2,1)}) %all-gather.15.cloned.1.call-update) | async-done | bytes 4194320 | tf_op jit(solution)/shard_map/all_gather | solution.py:66
  274.5 4.6 %convolution_convert_fusion.1 = bf16[256,2048]{1,0:T(8,128)(2,1)} fusion(bf16[1024,2048]{1,0:T(8,128)(2,1)} %all-gather.15.cloned.1.call-done, bf16[1024,1024]{1,0:T(8,128)(2,1)} %all-gather.13.cloned.1.call-done, s32[]{:T(128)S(6)} %select_n.2), kind=kOutput, calls=%fused_computation.14 | convolution fusion | flops 1074266112 | bytes 5767172 | tf_op jit(solution)/shard_map/dot_general | solution.py:68
  279.1 1.9 copy.26
  (42 shorter events, 3.1 us)
Async XLA Ops:
  8.0 123.2 %all-reduce.4.cloned.1.call-start = ((), (), s32[]{:S(2)}) async-start(), calls=%async_computation.3 | async-start | bytes 1048576 | tf_op jit(solution)/shard_map/psum | solution.py:60
  13.0 48.8 %copy-start.5 = (bf16[256,2048]{1,0:T(8,128)(2,1)}, bf16[256,2048]{1,0:T(8,128)(2,1)S(1)}, u32[]{:S(2)}) copy-start(bf16[256,2048]{1,0:T(8,128)(2,1)S(1)} %get-tuple-element.13) | copy-start | bytes 3145732
  61.9 23.2 %copy-start.4 = (bf16[256,1024]{1,0:T(8,128)(2,1)}, bf16[256,1024]{1,0:T(8,128)(2,1)S(1)}, u32[]{:S(2)}) copy-start(bf16[256,1024]{1,0:T(8,128)(2,1)S(1)} %all-reduce.7) | copy-start | bytes 1572868
  61.9 3.7 %copy-start = (bf16[2048,1024]{1,0:T(8,128)(2,1)S(1)}, bf16[2048,1024]{1,0:T(8,128)(2,1)}, u32[]{:S(2)}) copy-start(bf16[2048,1024]{1,0:T(8,128)(2,1)} %param.10) | copy-start | bytes 12582916
  65.6 4.7 %copy-start.6 = (f32[2048]{0:T(1024)S(1)}, f32[2048]{0:T(1024)}, u32[]{:S(2)}) copy-start(f32[2048]{0:T(1024)} %param.11) | copy-start | bytes 24580
  65.6 4.7 %copy-start.2 = (bf16[2048,1024]{1,0:T(8,128)(2,1)S(1)}, bf16[2048,1024]{1,0:T(8,128)(2,1)}, u32[]{:S(2)}) copy-start(bf16[2048,1024]{1,0:T(8,128)(2,1)} %param.9) | copy-start | bytes 12582916
  85.1 8.6 %copy-start.3 = (bf16[256,2048]{1,0:T(8,128)(2,1)}, bf16[256,2048]{1,0:T(8,128)(2,1)S(1)}, u32[]{:S(2)}) copy-start(bf16[256,2048]{1,0:T(8,128)(2,1)S(1)} %get-tuple-element.8) | copy-start | bytes 3145732
  85.1 3.9 %copy-start.1 = (bf16[2048,1024]{1,0:T(8,128)(2,1)S(1)}, bf16[2048,1024]{1,0:T(8,128)(2,1)}, u32[]{:S(2)}) copy-start(bf16[2048,1024]{1,0:T(8,128)(2,1)} %param.10) | copy-start | bytes 12582916
  93.6 39.1 %copy-start.8 = (f32[256,2048]{1,0:T(8,128)S(1)}, f32[256,2048]{1,0:T(8,128)}, u32[]{:S(2)}) copy-start(f32[256,2048]{1,0:T(8,128)} %get-tuple-element.14) | copy-start | bytes 6291460
  93.6 56.4 %all-gather.9.cloned.1.call-start = ((), (), s32[]{:S(2)}) async-start(), calls=%async_computation | async-start | bytes 2621440 | tf_op jit(solution)/shard_map/all_gather | solution.py:8
  94.2 59.9 %all-gather.11.cloned.1.call-start = ((), (), s32[]{:S(2)}) async-start(), calls=%async_computation.1 | async-start | bytes 5242880 | tf_op jit(solution)/shard_map/all_gather | solution.py:47
  94.8 83.2 %all-gather.17.cloned.1.call-start = ((), (), s32[]{:S(2)}) async-start(), calls=%async_computation.5 | async-start | bytes 2621440 | tf_op jit(solution)/shard_map/all_gather | solution.py:8
  131.2 82.8 %all-gather.19.cloned.1.call-start = ((), (), s32[]{:S(2)}) async-start(), calls=%async_computation.6 | async-start | bytes 5242880 | tf_op jit(solution)/shard_map/all_gather | solution.py:18
  132.0 106.1 %all-gather.13.cloned.1.call-start = ((), (), s32[]{:S(2)}) async-start(), calls=%async_computation.2 | async-start | bytes 2621440 | tf_op jit(solution)/shard_map/all_gather | solution.py:8
  132.7 141.8 %all-gather.15.cloned.1.call-start = ((), (), s32[]{:S(2)}) async-start(), calls=%async_computation.4 | async-start | bytes 5242880 | tf_op jit(solution)/shard_map/all_gather | solution.py:66
  137.8 141.4 %all-reduce.6.cloned.1.call-start = ((), (), s32[]{:S(2)}) async-start(), calls=%async_computation.7 | async-start | bytes 1048576 | tf_op jit(solution)/shard_map/psum | solution.py:65
  154.2 5.2 %copy-start.7 = (bf16[1024,2048]{1,0:T(8,128)(2,1)S(1)}, bf16[1024,2048]{1,0:T(8,128)(2,1)}, u32[]{:S(2)}) copy-start(bf16[1024,2048]{1,0:T(8,128)(2,1)} %all-gather.11.cloned.1.call-done) | copy-start | bytes 12582916
Sparse Core Ops, SparseCore 0:
  93.8 37.3 all-reduce.3
  150.1 38.3 all-reduce.5
Sparse Core Ops, SparseCore 1:
  96.3 21.2 all-gather.8
  119.5 34.6 all-gather.10
  155.6 22.4 all-gather.16
  179.6 34.3 all-gather.18
  215.6 22.4 all-gather.12
  240.2 34.3 all-gather.14
where the time goes:
time: 289 us; the launch traced here: 288 us
  waiting for transfers between devices  150 us (52%)
  blocking collectives  64.4 us (22%)
  matrix products  50.5 us (17%)
  between operations  15.8 us (5%)
  other arithmetic  5.57 us (2%)
    psum x1, blocking collectives, body(): head = lax.psum(partial_value, 'mp').astype(jnp.bfloat16)  45 us
    all_gather x1, waiting for transfers between devices, body(): pre_all = lax.all_gather(grad_pre, 'dp', axis=0, tiled=True)  36.5 us
    psum x1, waiting for transfers between devices, body(): grad_head = lax.psum(grad_term.astype(jnp.bfloat16), 'mp')  36.3 us
    all_gather x1, waiting for transfers between devices, body(): hidden_all = lax.all_gather(hidden, 'dp', axis=0, tiled=True)  35.9 us
    all_gather x3, waiting for transfers between devices, my_columns(): gathered = lax.all_gather(rows, axis, axis=0, tiled=True)  34.5 us
    all_gather x1, blocking collectives, body(): stats = lax.all_gather(jnp.stack([local_top, local_total]), 'mp')  11.9 us
    psum x1, blocking collectives, body(): counts = lax.psum(jnp.sum(resp, axis=0), 'dp')  7.52 us
  transfers between devices with their start and end apart: 8, of which 6 were waited for; matrix products, arithmetic and copies ran while one was open for 10% of the time, Pallas kernels for 0%

commit v1 on v0

--- a/solution.py
+++ b/solution.py
@@ -63,7 +63,12 @@
     grad_pre = (back * sigma * (1.0 + pre * (1.0 - sigma))).astype(jnp.bfloat16)
     embed_term = lax.dot_general(grad_pre, w_in, contract_cols, preferred_element_type=jnp.float32)
     grad_embed = lax.psum(embed_term.astype(jnp.bfloat16), "mp")
-    pre_all = lax.all_gather(grad_pre, "dp", axis=0, tiled=True)
+    ring = [grad_pre]
+    for hop in range(3):
+        ring.append(lax.ppermute(ring[-1], "dp", [(dev, (dev + 1) % 4) for dev in range(4)]))
+    pre_all = jnp.roll(
+        jnp.concatenate(ring[::-1], axis=0), (lax.axis_index("dp") + 1) * ring[0].shape[0], axis=0
+    )
     grad_cols = my_columns(grad_head, "dp")
     grad_w_in = lax.dot_general(
         emb_cols, pre_all, contract_rows, preferred_element_type=jnp.float32

time: 289 us -> 264 us (0.913)
  waiting for transfers between devices: 150 us -> 106 us
  local copies, waits for them, and re-layouts: 1.92 us -> 13 us
  blocking collectives: 64.4 us -> 72.9 us
    ppermute x0 -> x3, waiting for transfers between devices: none -> 50.2 us  [body(): lax.ppermute(ring[-1], 'dp', [(dev, (dev + 1) % 4) for dev in range(4)])]
    all_gather x1 -> x0, waiting for transfers between devices: 36.5 us -> none  [body(): pre_all = lax.all_gather(grad_pre, 'dp', axis=0, tiled=True)]
    all_gather x3, waiting for transfers between devices: 34.5 us -> 0.01 us  [my_columns(): gathered = lax.all_gather(rows, axis, axis=0, tiled=True)]
    all_gather x1, waiting for transfers between devices: 35.9 us -> 17.6 us  [body(): hidden_all = lax.all_gather(hidden, 'dp', axis=0, tiled=True)]
    unnamed x19 -> x26, local copies, waits for them, and re-layouts: 1.92 us -> 11.9 us
    psum x1, blocking collectives: 7.52 us -> 16 us  [body(): counts = lax.psum(jnp.sum(resp, axis=0), 'dp')]
    all_gather x1, waiting for transfers between devices: 4.16 us -> 0.01 us  [body(): resp_all = lax.all_gather(resp_b, 'dp', axis=0, tiled=True)]
  transfers between devices with their start and end apart: 8 -> 10, of which waited for: 6 -> 4; matrix products, arithmetic and copies ran while one was open for 10% -> 14% of each run, Pallas kernels for 0% -> 0%
where the time goes in v1:
time: 264 us
  waiting for transfers between devices  106 us (40%)
  blocking collectives  72.9 us (28%)
  matrix products  49.9 us (19%)
  between operations  15.9 us (6%)
  local copies, waits for them, and re-layouts  13 us (5%)
  other arithmetic  5.52 us (2%)
    ppermute x3, waiting for transfers between devices, body(): lax.ppermute(ring[-1], 'dp', [(dev, (dev + 1) % 4) for dev in range(4)])  50.2 us
    psum x1, blocking collectives, body(): head = lax.psum(partial_value, 'mp').astype(jnp.bfloat16)  45 us
    psum x1, waiting for transfers between devices, body(): grad_head = lax.psum(grad_term.astype(jnp.bfloat16), 'mp')  35.8 us
    all_gather x1, waiting for transfers between devices, body(): hidden_all = lax.all_gather(hidden, 'dp', axis=0, tiled=True)  17.6 us
    psum x1, blocking collectives, body(): counts = lax.psum(jnp.sum(resp, axis=0), 'dp')  16 us
    unnamed x26, local copies, waits for them, and re-layouts  11.9 us
    all_gather x1, blocking collectives, body(): stats = lax.all_gather(jnp.stack([local_top, local_total]), 'mp')  11.9 us
    dot_general x1, matrix products, body(): lax.dot_general(squares_cols, resp_all, contract_rows, preferred_element_...  5.88 us
  transfers between devices with their start and end apart: 10, of which 4 were waited for; matrix products, arithmetic and copies ran while one was open for 14% of the time, Pallas kernels for 0%

profile of v1, /device:TPU:0, one launch (start us, length us, event | category | flops | bytes accessed | tf_op | source)
XLA Modules:
  0.0 263.7 jit_solution(9885129190286161165)
XLA Ops:
  8.0 5.0 %multiply_convert_fusion = (bf16[256,2048]{1,0:T(8,128)(2,1)S(1)}, f32[256,2048]{1,0:T(8,128)}) fusion(bf16[256,1024]{1,0:T(8,128)(2,1)} %param.6, bf16[1024,2048]{1,0:T(8,128)(2,1)} %param.7), kind=kOutput, calls=%fused_computation.19 | convolution fusion | flops 1076363264 | bytes 7864320 | tf_op jit(solution)/shard_map/dot_general | solution.py:16
  13.0 3.8 %fusion.39 = f32[256,1024]{1,0:T(8,128)S(1)} fusion(bf16[256,2048]{1,0:T(8,128)(2,1)S(1)} %get-tuple-element.13, bf16[2048,1024]{1,0:T(8,128)(2,1)} %param.8), kind=kOutput, calls=%fused_computation.60 | convolution fusion | flops 1073741824 | bytes 6291456 | tf_op jit(solution)/shard_map/dot_general | solution.py:20
  16.9 45.0 %all-reduce.7 = bf16[256,1024]{1,0:T(8,128)(2,1)S(1)} all-reduce(f32[256,1024]{1,0:T(8,128)S(1)} %fusion.39), channel_id=1, replica_groups=mesh['parts'=2,'mp'=4,'dp'=4] {'mp'}, use_global_device_ids=true, to_apply=%region_2.3 | all-reduce | flops 262144 | bytes 1572864 | tf_op jit(solution)/shard_map/psum | solution.py:21
  61.9 3.7 %convolution_multiply_fusion.1 = f32[256,2048]{1,0:T(8,128)S(1)} fusion(bf16[2048,1024]{1,0:T(8,128)(2,1)} %param.10, bf16[256,1024]{1,0:T(8,128)(2,1)S(1)} %all-reduce.7), kind=kOutput, calls=%fused_computation.10 | convolution fusion | flops 1075052544 | bytes 6815744 | tf_op jit(solution)/shard_map/dot_general | solution.py:35
  65.6 4.6 %fusion = (f32[2048]{0:T(1024)S(1)}, f32[2048]{0:T(1024)S(1)}) fusion(bf16[2048,1024]{1,0:T(8,128)(2,1)S(1)} %copy-done, bf16[2048,1024]{1,0:T(8,128)(2,1)} %param.9), kind=kLoop, calls=%fused_computation.4 | loop fusion | flops 12578816 | bytes 8404992 | tf_op jit(solution)/shard_map/reduce_sum | solution.py:29
  70.3 1.9 fusion.38
  72.6 11.9 %all-gather.1 = f32[4,2,256]{2,1,0:T(2,128)S(1)} all-gather(f32[1,2,256]{2,1,0:T(2,128)S(1)} %maximum_bitcast_fusion), channel_id=2, replica_groups=mesh['parts'=2,'mp'=4,'dp'=4] {'mp'}, dimensions={0}, use_global_device_ids=true | all-gather | bytes 10240 | tf_op jit(solution)/shard_map/all_gather | solution.py:40
  85.0 3.9 %convolution_multiply_fusion.2 = f32[256,1024]{1,0:T(8,128)S(1)} fusion(bf16[256,2048]{1,0:T(8,128)(2,1)S(1)} %get-tuple-element.8, bf16[2048,1024]{1,0:T(8,128)(2,1)} %param.10, bf16[256,1024]{1,0:T(8,128)(2,1)S(1)} %all-reduce.7), kind=kOutput, calls=%fused_computation.24 | convolution fusion | flops 1074266112 | bytes 6815744 | tf_op jit(solution)/shard_map/dot_general | solution.py:57
  89.0 4.6 %fusion.19 = bf16[256,1024]{1,0:T(8,128)(2,1)} fusion(f32[256,1024]{1,0:T(8,128)S(1)} %convolution_multiply_fusion.2, bf16[256,2048]{1,0:T(8,128)(2,1)S(1)} %get-tuple-element.8, bf16[2048,1024]{1,0:T(8,128)(2,1)S(1)} %copy-done.1, bf16[2048,1024]{1,0:T(8,128)(2,1)} %param.9), kind=kOutput, calls=%fused_computation.27 | convolution fusion | flops 1082654720 | bytes 11010048 | tf_op jit(solution)/shard_map/dot_general | solution.py:58
  95.4 35.8 %all-reduce.4.cloned.1.call-done = bf16[256,1024]{1,0:T(8,128)(2,1)} async-done(((bf16[256,1024]{1,0:T(8,128)(2,1)}), bf16[256,1024]{1,0:T(8,128)(2,1)}) %all-reduce.4.cloned.1.call-update) | async-done | bytes 524304 | tf_op jit(solution)/shard_map/psum | solution.py:60
  132.0 4.0 %fusion.10 = bf16[256,2048]{1,0:T(8,128)(2,1)S(1)} fusion(bf16[256,1024]{1,0:T(8,128)(2,1)} %all-reduce.4.cloned.1.call-done, bf16[2048,1024]{1,0:T(8,128)(2,1)} %param.8, f32[256,2048]{1,0:T(8,128)S(1)} %copy-done.8), kind=kOutput, calls=%fused_computation.15 | convolution fusion | flops 1078460416 | bytes 7864320 | tf_op jit(solution)/shard_map/dot_general | solution.py:61
  136.2 14.9 %collective-permute-done = bf16[256,2048]{1,0:T(8,128)(2,1)S(1)} collective-permute-done((bf16[256,2048]{1,0:T(8,128)(2,1)S(1)}, bf16[256,2048]{1,0:T(8,128)(2,1)S(1)}, u32[]{:S(2)}, u32[]{:S(2)}) %collective-permute-start) | collective-permute-done | bytes 1048608 | tf_op jit(solution)/shard_map/ppermute | solution.py:68
  151.1 35.3 %collective-permute-done.1 = bf16[256,2048]{1,0:T(8,128)(2,1)S(1)} collective-permute-done((bf16[256,2048]{1,0:T(8,128)(2,1)S(1)}, bf16[256,2048]{1,0:T(8,128)(2,1)S(1)}, u32[]{:S(2)}, u32[]{:S(2)}) %collective-permute-start.1) | collective-permute-done | bytes 1048608 | tf_op jit(solution)/shard_map/ppermute | solution.py:68
  186.5 16.0 %psum.29 = f32[2048]{0:T(1024)} all-reduce(f32[2048]{0:T(1024)S(1)} %get-tuple-element.9), channel_id=1, replica_groups=mesh['parts'=2,'mp'=4,'dp'=4] {'dp'}, use_global_device_ids=true, to_apply=%region_8.9 | all-reduce | flops 2048 | bytes 16384 | tf_op jit(solution)/shard_map/psum | solution.py:46
  202.5 4.3 %convolution_convert_fusion.1 = bf16[256,1024]{1,0:T(8,128)(2,1)} fusion(bf16[256,2048]{1,0:T(8,128)(2,1)S(1)} %fusion.10, bf16[1024,2048]{1,0:T(8,128)(2,1)} %param.7), kind=kOutput, calls=%fused_computation.28 | convolution fusion | flops 1074003968 | bytes 5767168 | tf_op jit(solution)/shard_map/dot_general | solution.py:64
  206.8 2.3 constant_dynamic-update-slice_fusion.7
  209.1 1.1 constant_dynamic-update-slice_fusion.6
  212.3 2.4 constant_dynamic-update-slice_fusion.3
  217.9 4.6 %fusion.7 = bf16[256,2048]{1,0:T(8,128)(2,1)} fusion(bf16[2048,2048]{1,0:T(8,128)(2,1)} %constant_dynamic-update-slice_fusion, s32[]{:T(128)S(6)} %select_n.20, bf16[1024,1024]{1,0:T(8,128)(2,1)} %all-gather.12.cloned.1.call-done, s32[]{:T(128)S(6)} %select_n.18), kind=kOutput, calls=%fused_computation.14 | convolution fusion | flops 1074266112 | bytes 5767176 | tf_op jit(solution)/shard_map/dot_general | solution.py:73
  222.5 5.9 %fusion.23 = f32[256,2048]{1,0:T(8,128)} fusion(bf16[1024,2048]{1,0:T(8,128)(2,1)} %all-gather.10.cloned.1.call-done, bf16[1024,1024]{1,0:T(8,128)(2,1)} %all-gather.8.cloned.1.call-done, s32[]{:T(128)S(6)} %select_n.18), kind=kOutput, calls=%fused_computation.31 | convolution fusion | flops 1074528256 | bytes 6815748 | tf_op jit(solution)/shard_map/dot_general | solution.py:54
  228.4 3.6 %fusion.28 = f32[256,2048]{1,0:T(8,128)} fusion(bf16[1024,2048]{1,0:T(8,128)(2,1)S(1)} %copy-done.7, bf16[1024,1024]{1,0:T(8,128)(2,1)} %all-gather.8.cloned.1.call-done, s32[]{:T(128)S(6)} %select_n.18), kind=kOutput, calls=%fused_computation.35 | convolution fusion | flops 1073741824 | bytes 6815748 | tf_op jit(solution)/shard_map/dot_general | solution.py:51
  232.1 17.6 %all-gather.16.cloned.1.call-done = bf16[1024,2048]{1,0:T(8,128)(2,1)} async-done(((bf16[256,2048]{1,0:T(8,128)(2,1)}), bf16[1024,2048]{1,0:T(8,128)(2,1)}) %all-gather.16.cloned.1.call-update) | async-done | bytes 4194320 | tf_op jit(solution)/shard_map/all_gather | solution.py:18
  249.6 4.6 %convolution_convert_fusion = bf16[256,2048]{1,0:T(8,128)(2,1)} fusion(bf16[1024,2048]{1,0:T(8,128)(2,1)} %all-gather.16.cloned.1.call-done, bf16[1024,1024]{1,0:T(8,128)(2,1)} %all-gather.14.cloned.1.call-done, s32[]{:T(128)S(6)} %select_n.18), kind=kOutput, calls=%fused_computation.16 | convolution fusion | flops 1074266112 | bytes 5767172 | tf_op jit(solution)/shard_map/dot_general | solution.py:76
  254.2 1.9 copy.33
  (53 shorter events, 9.1 us)
Async XLA Ops:
  8.0 123.1 %all-reduce.4.cloned.1.call-start = ((), (), s32[]{:S(2)}) async-start(), calls=%async_computation.3 | async-start | bytes 1048576 | tf_op jit(solution)/shard_map/psum | solution.py:60
  13.0 48.8 %copy-start.5 = (bf16[256,2048]{1,0:T(8,128)(2,1)}, bf16[256,2048]{1,0:T(8,128)(2,1)S(1)}, u32[]{:S(2)}) copy-start(bf16[256,2048]{1,0:T(8,128)(2,1)S(1)} %get-tuple-element.13) | copy-start | bytes 3145732
  61.9 23.2 %copy-start.4 = (bf16[256,1024]{1,0:T(8,128)(2,1)}, bf16[256,1024]{1,0:T(8,128)(2,1)S(1)}, u32[]{:S(2)}) copy-start(bf16[256,1024]{1,0:T(8,128)(2,1)S(1)} %all-reduce.7) | copy-start | bytes 1572868
  61.9 3.7 %copy-start = (bf16[2048,1024]{1,0:T(8,128)(2,1)S(1)}, bf16[2048,1024]{1,0:T(8,128)(2,1)}, u32[]{:S(2)}) copy-start(bf16[2048,1024]{1,0:T(8,128)(2,1)} %param.10) | copy-start | bytes 12582916
  65.6 4.6 %copy-start.6 = (f32[2048]{0:T(1024)S(1)}, f32[2048]{0:T(1024)}, u32[]{:S(2)}) copy-start(f32[2048]{0:T(1024)} %param.11) | copy-start | bytes 24580
  65.6 4.7 %copy-start.2 = (bf16[2048,1024]{1,0:T(8,128)(2,1)S(1)}, bf16[2048,1024]{1,0:T(8,128)(2,1)}, u32[]{:S(2)}) copy-start(bf16[2048,1024]{1,0:T(8,128)(2,1)} %param.9) | copy-start | bytes 12582916
  85.0 8.6 %copy-start.3 = (bf16[256,2048]{1,0:T(8,128)(2,1)}, bf16[256,2048]{1,0:T(8,128)(2,1)S(1)}, u32[]{:S(2)}) copy-start(bf16[256,2048]{1,0:T(8,128)(2,1)S(1)} %get-tuple-element.8) | copy-start | bytes 3145732
  85.0 3.9 %copy-start.1 = (bf16[2048,1024]{1,0:T(8,128)(2,1)S(1)}, bf16[2048,1024]{1,0:T(8,128)(2,1)}, u32[]{:S(2)}) copy-start(bf16[2048,1024]{1,0:T(8,128)(2,1)} %param.10) | copy-start | bytes 12582916
  93.6 38.4 %copy-start.8 = (f32[256,2048]{1,0:T(8,128)S(1)}, f32[256,2048]{1,0:T(8,128)}, u32[]{:S(2)}) copy-start(f32[256,2048]{1,0:T(8,128)} %get-tuple-element.14) | copy-start | bytes 6291460
  93.6 124.3 %all-gather.12.cloned.1.call-start = ((), (), s32[]{:S(2)}) async-start(), calls=%async_computation.2 | async-start | bytes 2621440 | tf_op jit(solution)/shard_map/all_gather | solution.py:8
  94.2 128.4 %all-gather.8.cloned.1.call-start = ((), (), s32[]{:S(2)}) async-start(), calls=%async_computation | async-start | bytes 2621440 | tf_op jit(solution)/shard_map/all_gather | solution.py:8
  94.8 127.8 %all-gather.10.cloned.1.call-start = ((), (), s32[]{:S(2)}) async-start(), calls=%async_computation.1 | async-start | bytes 5242880 | tf_op jit(solution)/shard_map/all_gather | solution.py:47
  95.3 136.7 %all-gather.14.cloned.1.call-start = ((), (), s32[]{:S(2)}) async-start(), calls=%async_computation.4 | async-start | bytes 2621440 | tf_op jit(solution)/shard_map/all_gather | solution.py:8
  131.2 118.4 %all-gather.16.cloned.1.call-start = ((), (), s32[]{:S(2)}) async-start(), calls=%async_computation.5 | async-start | bytes 5242880 | tf_op jit(solution)/shard_map/all_gather | solution.py:18
  131.9 122.3 %all-reduce.6.cloned.1.call-start = ((), (), s32[]{:S(2)}) async-start(), calls=%async_computation.6 | async-start | bytes 1048576 | tf_op jit(solution)/shard_map/psum | solution.py:65
  136.0 15.1 %collective-permute-start = (bf16[256,2048]{1,0:T(8,128)(2,1)S(1)}, bf16[256,2048]{1,0:T(8,128)(2,1)S(1)}, u32[]{:S(2)}, u32[]{:S(2)}) collective-permute-start(bf16[256,2048]{1,0:T(8,128)(2,1)S(1)} %fusion.10), channel_id=1, source_target_pairs={{0,1},{1,2},{2,3},{3,0},{4,5},{5,6},{6,7},{7,4},{8,9},{9,10},{10,1... | collective-permute-start | bytes 3145736 | tf_op jit(solution)/shard_map/ppermute | solution.py:68
  151.1 35.4 %collective-permute-start.1 = (bf16[256,2048]{1,0:T(8,128)(2,1)S(1)}, bf16[256,2048]{1,0:T(8,128)(2,1)S(1)}, u32[]{:S(2)}, u32[]{:S(2)}) collective-permute-start(bf16[256,2048]{1,0:T(8,128)(2,1)S(1)} %collective-permute-done), channel_id=1, source_target_pairs={{0,1},{1,2},{2,3},{3,0},{4,5},{5,6},{6,7},{7,4},{8,9},{9,10},{10,1... | collective-permute-start | bytes 3145736 | tf_op jit(solution)/shard_map/ppermute | solution.py:68
  186.5 20.3 %collective-permute-start.2 = (bf16[256,2048]{1,0:T(8,128)(2,1)S(1)}, bf16[256,2048]{1,0:T(8,128)(2,1)}, u32[]{:S(2)}, u32[]{:S(2)}) collective-permute-start(bf16[256,2048]{1,0:T(8,128)(2,1)S(1)} %collective-permute-done.1), channel_id=1, source_target_pairs={{0,1},{1,2},{2,3},{3,0},{4,5},{5,6},{6,7},{7,4},{8,9},{9,10},{10,1... | collective-permute-start | bytes 3145736 | tf_op jit(solution)/shard_map/ppermute | solution.py:68
  222.5 5.9 %copy-start.7 = (bf16[1024,2048]{1,0:T(8,128)(2,1)S(1)}, bf16[1024,2048]{1,0:T(8,128)(2,1)}, u32[]{:S(2)}) copy-start(bf16[1024,2048]{1,0:T(8,128)(2,1)} %all-gather.10.cloned.1.call-done) | copy-start | bytes 12582916
Sparse Core Ops, SparseCore 0:
  93.7 37.3 all-reduce.3
  206.9 39.6 all-reduce.5
Sparse Core Ops, SparseCore 1:
  95.6 21.2 all-gather.11
  118.9 22.9 all-gather.7
  143.9 45.5 all-gather.9
  191.0 22.7 all-gather.13
  215.3 34.3 all-gather.15
